TPU v7x, 32 devices: a whole 2x2x4 slice. The times are simulated.
32 devices in a mesh: term: 8 (over z, y), sec: 4 (over x, core).
Axes of the slice: x: 2, y: 2, z: 4, core: 2. Of those that a mesh axis runs over, the one named last changes fastest.
Arguments:
- state: bfloat16 [4, 768, 768], P('sec'), may hold values from -6 to 6
- left_environment: bfloat16 [8, 4, 768, 768], P('term', 'sec'), may hold values from -0.21875 to 0.21875
- right_environment: bfloat16 [8, 4, 768, 768], P('term', 'sec'), may hold values from -0.21875 to 0.21875
- site_blocks: bfloat16 [4, 768, 768], P('sec'), may hold values from -3 to 3
- sector_sizes: int32 [4], replicated, may hold values from 192 to 768, as said below
- term_shift: int32 [8], P('term'), may hold values from -1 to 1
Outputs:
- applied: float32 [4, 768, 768], P('sec', 'term')
- new_left: bfloat16 [8, 4, 768, 768], P('term', 'sec')
Inputs may be any that keep to these rules, and one draw needn't show every extreme that they name: `sector_sizes`: every sector holds at least 192 states and the largest sector holds exactly 768.
All inputs are finite; a program needn't handle non-finite values.
Results may differ from a plain program's by a relative error of at most 0.0049.
Values may be sent and summed in bfloat16 or wider, within the bound.
A program may use at most 64 MiB of HBM per device.

v0:
```python
import jax
import jax.numpy as jnp
from jax import lax
from jax.sharding import PartitionSpec as P


def passed_along(block, axis, distance):
    devices = range(lax.axis_size(axis))
    route = [(i - distance, i) for i in devices if i - distance in devices]
    return lax.ppermute(block, axis, route)


def shards(state, left_environment, right_environment, site_blocks, sector_sizes, term_shift):
    width = state.shape[1]
    sector = lax.axis_index("sec")
    sector_count = lax.axis_size("sec")
    charge_shift = term_shift[0]
    sector_ids = jnp.arange(sector_count, dtype=jnp.int32)
    own_size = jnp.sum(jnp.where(sector_ids == sector, sector_sizes, 0))
    source_size = jnp.sum(jnp.where(sector_ids == sector + charge_shift, sector_sizes, 0))
    row_index = jnp.arange(width, dtype=jnp.int32)
    own_mask = row_index < own_size
    source_mask = row_index < source_size
    own_square = own_mask[:, None] & own_mask[None, :]
    zero_block = jnp.zeros((width, width), jnp.bfloat16)
    state_own = jnp.where(own_square, state[0], zero_block)
    site_own = jnp.where(own_square, site_blocks[0], zero_block)
    below_state, below_site = passed_along((state_own, site_own), "sec", 1)
    above_state, above_site = passed_along((state_own, site_own), "sec", -1)
    source_state = jnp.where(
        charge_shift == 1, above_state, jnp.where(charge_shift == -1, below_state, state_own)
    )
    source_site = jnp.where(
        charge_shift == 1, above_site, jnp.where(charge_shift == -1, below_site, site_own)
    )
    left_masked = jnp.where(
        own_mask[:, None] & source_mask[None, :], left_environment[0, 0], zero_block
    )
    right_masked = jnp.where(
        source_mask[:, None] & own_mask[None, :], right_environment[0, 0], zero_block
    )
    mixed_block = jnp.dot(source_state, right_masked, preferred_element_type=jnp.float32).astype(
        jnp.bfloat16
    )
    applied = lax.psum_scatter(
        jnp.dot(left_masked, mixed_block, preferred_element_type=jnp.float32),
        "term",
        scatter_dimension=0,
        tiled=True,
    )
    carried = jnp.dot(left_masked, source_site, preferred_element_type=jnp.float32).astype(
        jnp.bfloat16
    )
    renewed = lax.dot_general(
        site_own, carried, (((0,), (0,)), ((), ())), preferred_element_type=jnp.float32
    )
    return (applied[None], renewed.astype(jnp.bfloat16)[None, None])


def solution(mesh):
    placed = (
        P("sec", None, None),
        P("term", "sec", None, None),
        P("term", "sec", None, None),
        P("sec", None, None),
        P(),
        P("term"),
    )
    return jax.shard_map(
        shards,
        mesh=mesh,
        in_specs=placed,
        out_specs=(P("sec", "term", None), P("term", "sec", None, None)),
        check_vma=False,
    )
```

profile of v0, /device:TPU:1, one launch (start us, length us, event | category | flops | bytes accessed | tf_op | source)
XLA Modules:
  0.0 115.1 jit_solution(11896368735799729507)
XLA Ops:
  7.2 0.0 reduce-scatter.2.cloned.1.call-start
  7.9 1.3 %fusion.25 = (s32[]{:T(128)}, s32[]{:T(128)}) fusion(s32[4]{0:T(128)} %param.10, s32[]{:T(128)S(6)} %add.5, s32[]{:T(128)S(6)} %axis_index.12), kind=kLoop, calls=%fused_computation.26 | loop fusion | flops 22 | bytes 32 | tf_op jit(solution)/shard_map/reduce_sum | solution.py:20
  9.2 0.6 iota_compare_fusion.1
  9.8 0.0 copy-start
  9.8 2.3 %and_select_fusion = (bf16[768,768]{1,0:T(8,128)(2,1)S(1)}, bf16[768,768]{1,0:T(8,128)(2,1)S(1)}) fusion(bf16[1,768,768]{2,1,0:T(8,128)(2,1)} %param.9, pred[768]{0:T(1024)(128)(4,1)S(1)} %iota_compare_fusion.1, bf16[1,768,768]{2,1,0:T(8,128)(2,1)} %param.6), kind=kLoop, calls=%fused_computation | loop fusion | flops 1769472 | bytes 4719360 | tf_op jit(solution)/shard_map/jit(_where)/select_n | solution.py:27
  12.1 4.5 %collective-permute-start.1 = (bf16[768,768]{1,0:T(8,128)(2,1)S(1)}, bf16[768,768]{1,0:T(8,128)(2,1)}, u32[]{:S(2)}, u32[]{:S(2)}) collective-permute-start(bf16[768,768]{1,0:T(8,128)(2,1)S(1)} %get-tuple-element.5), channel_id=1, source_target_pairs={{0,1},{1,2},{2,3},{4,5},{5,6},{6,7},{8,9},{9,10},{10,11},{12,13},{... | collective-permute-start | bytes 3538952 | tf_op jit(solution)/shard_map/ppermute | solution.py:10
  16.6 1.9 %collective-permute-start = (bf16[768,768]{1,0:T(8,128)(2,1)S(1)}, bf16[768,768]{1,0:T(8,128)(2,1)}, u32[]{:S(2)}, u32[]{:S(2)}) collective-permute-start(bf16[768,768]{1,0:T(8,128)(2,1)S(1)} %get-tuple-element.5), channel_id=1, source_target_pairs={{1,0},{2,1},{3,2},{5,4},{6,5},{7,6},{9,8},{10,9},{11,10},{13,12},{... | collective-permute-start | bytes 3538952 | tf_op jit(solution)/shard_map/ppermute | solution.py:10
  18.6 0.7 iota_compare_fusion
  19.2 10.5 %collective-permute-done.1 = bf16[768,768]{1,0:T(8,128)(2,1)} collective-permute-done((bf16[768,768]{1,0:T(8,128)(2,1)S(1)}, bf16[768,768]{1,0:T(8,128)(2,1)}, u32[]{:S(2)}, u32[]{:S(2)}) %collective-permute-start.1) | collective-permute-done | bytes 1179680 | tf_op jit(solution)/shard_map/ppermute | solution.py:10
  29.8 4.5 %collective-permute-done = bf16[768,768]{1,0:T(8,128)(2,1)} collective-permute-done((bf16[768,768]{1,0:T(8,128)(2,1)S(1)}, bf16[768,768]{1,0:T(8,128)(2,1)}, u32[]{:S(2)}, u32[]{:S(2)}) %collective-permute-start) | collective-permute-done | bytes 1179680 | tf_op jit(solution)/shard_map/ppermute | solution.py:10
  34.3 0.0 copy-done
  34.3 5.7 %fusion.6 = f32[768,768]{1,0:T(8,128)} fusion(bf16[1,1,768,768]{3,2,1,0:T(8,128)(2,1)} %param.8, bf16[768,768]{1,0:T(8,128)(2,1)} %collective-permute-done, bf16[768,768]{1,0:T(8,128)(2,1)} %collective-permute-done.1, pred[]{:T(512)S(6)} %eq.25, pred[768]{0:T(1024)(128)(4,1)S(1)} %iota_compare_fusion.1, pred[]{:T(512)S(6)} %eq.24, ...), kind=kOutput, calls=%fused_computation.12 | convolution fusion | flops 1817247744 | bytes 8259074 | tf_op jit(solution)/shard_map/dot_general | solution.py:46
  39.9 0.0 copy-start.1
  40.0 0.0 copy-start.2
  40.0 0.0 reduce-scatter.2.cloned.1.call-update
  40.0 2.1 %collective-permute-start.3 = (bf16[768,768]{1,0:T(8,128)(2,1)S(1)}, bf16[768,768]{1,0:T(8,128)(2,1)S(1)}, u32[]{:S(2)}, u32[]{:S(2)}) collective-permute-start(bf16[768,768]{1,0:T(8,128)(2,1)S(1)} %get-tuple-element.4), channel_id=1, source_target_pairs={{0,1},{1,2},{2,3},{4,5},{5,6},{6,7},{8,9},{9,10},{10,11},{12,13},{... | collective-permute-start | bytes 3538952 | tf_op jit(solution)/shard_map/ppermute | solution.py:10
  42.0 2.5 %collective-permute-start.2 = (bf16[768,768]{1,0:T(8,128)(2,1)S(1)}, bf16[768,768]{1,0:T(8,128)(2,1)}, u32[]{:S(2)}, u32[]{:S(2)}) collective-permute-start(bf16[768,768]{1,0:T(8,128)(2,1)S(1)} %get-tuple-element.4), channel_id=1, source_target_pairs={{1,0},{2,1},{3,2},{5,4},{6,5},{7,6},{9,8},{10,9},{11,10},{13,12},{... | collective-permute-start | bytes 3538952 | tf_op jit(solution)/shard_map/ppermute | solution.py:10
  44.5 10.6 %collective-permute-done.3 = bf16[768,768]{1,0:T(8,128)(2,1)S(1)} collective-permute-done((bf16[768,768]{1,0:T(8,128)(2,1)S(1)}, bf16[768,768]{1,0:T(8,128)(2,1)S(1)}, u32[]{:S(2)}, u32[]{:S(2)}) %collective-permute-start.3) | collective-permute-done | bytes 1179680 | tf_op jit(solution)/shard_map/ppermute | solution.py:10
  55.2 0.0 copy-start.3
  55.2 1.0 copy-done.3
  56.2 3.8 %collective-permute-done.2 = bf16[768,768]{1,0:T(8,128)(2,1)} collective-permute-done((bf16[768,768]{1,0:T(8,128)(2,1)S(1)}, bf16[768,768]{1,0:T(8,128)(2,1)}, u32[]{:S(2)}, u32[]{:S(2)}) %collective-permute-start.2) | collective-permute-done | bytes 1179680 | tf_op jit(solution)/shard_map/ppermute | solution.py:10
  60.0 0.0 copy-done.1
  60.0 0.0 copy-done.2
  60.0 6.0 %fusion = bf16[1,1,768,768]{3,2,1,0:T(8,128)(2,1)} fusion(bf16[768,768]{1,0:T(8,128)(2,1)} %collective-permute-done.2, bf16[768,768]{1,0:T(8,128)(2,1)} %copy-done.3, pred[]{:T(512)S(6)} %eq.25, pred[]{:T(512)S(6)} %eq.24, bf16[1,1,768,768]{3,2,1,0:T(8,128)(2,1)S(1)} %copy-done.2, pred[768]{0:T(1024)(128)(4,1)S(1)} %iota_compare_fusion, ...), kind=kOutput, calls=%fused_computation.7 | convolution fusion | flops 1817837568 | bytes 5899778 | tf_op jit(solution)/shard_map/dot_general | solution.py:54
  66.0 42.3 %reduce-scatter.2.cloned.1.call-done = f32[96,768]{1,0:T(8,128)} async-done(((f32[768,768]{1,0:T(8,128)}), f32[96,768]{1,0:T(8,128)}) %reduce-scatter.2.cloned.1.call-update) | async-done | bytes 294928 | tf_op jit(solution)/shard_map/reduce_scatter | solution.py:45
Async XLA Ops:
  7.2 101.1 %reduce-scatter.2.cloned.1.call-start = ((), (), s32[]{:S(2)}) async-start(), calls=%async_computation.1 | async-start | bytes 2654208 | tf_op jit(solution)/shard_map/reduce_scatter | solution.py:45
  9.8 24.5 %copy-start = (bf16[1,768,768]{2,1,0:T(8,128)(2,1)S(1)}, bf16[1,768,768]{2,1,0:T(8,128)(2,1)}, u32[]{:S(2)}) copy-start(bf16[1,768,768]{2,1,0:T(8,128)(2,1)} %param.6) | copy-start | bytes 3538948
  12.1 17.6 %collective-permute-start.1 = (bf16[768,768]{1,0:T(8,128)(2,1)S(1)}, bf16[768,768]{1,0:T(8,128)(2,1)}, u32[]{:S(2)}, u32[]{:S(2)}) collective-permute-start(bf16[768,768]{1,0:T(8,128)(2,1)S(1)} %get-tuple-element.5), channel_id=1, source_target_pairs={{0,1},{1,2},{2,3},{4,5},{5,6},{6,7},{8,9},{9,10},{10,11},{12,13},{... | collective-permute-start | bytes 3538952 | tf_op jit(solution)/shard_map/ppermute | solution.py:10
  16.6 17.6 %collective-permute-start = (bf16[768,768]{1,0:T(8,128)(2,1)S(1)}, bf16[768,768]{1,0:T(8,128)(2,1)}, u32[]{:S(2)}, u32[]{:S(2)}) collective-permute-start(bf16[768,768]{1,0:T(8,128)(2,1)S(1)} %get-tuple-element.5), channel_id=1, source_target_pairs={{1,0},{2,1},{3,2},{5,4},{6,5},{7,6},{9,8},{10,9},{11,10},{13,12},{... | collective-permute-start | bytes 3538952 | tf_op jit(solution)/shard_map/ppermute | solution.py:10
  39.9 20.0 %copy-start.1 = (bf16[1,768,768]{2,1,0:T(8,128)(2,1)S(1)}, bf16[1,768,768]{2,1,0:T(8,128)(2,1)}, u32[]{:S(2)}) copy-start(bf16[1,768,768]{2,1,0:T(8,128)(2,1)} %param.9) | copy-start | bytes 3538948
  40.0 20.0 %copy-start.2 = (bf16[1,1,768,768]{3,2,1,0:T(8,128)(2,1)S(1)}, bf16[1,1,768,768]{3,2,1,0:T(8,128)(2,1)}, u32[]{:S(2)}) copy-start(bf16[1,1,768,768]{3,2,1,0:T(8,128)(2,1)} %param.7) | copy-start | bytes 3538948
  40.0 15.2 %collective-permute-start.3 = (bf16[768,768]{1,0:T(8,128)(2,1)S(1)}, bf16[768,768]{1,0:T(8,128)(2,1)S(1)}, u32[]{:S(2)}, u32[]{:S(2)}) collective-permute-start(bf16[768,768]{1,0:T(8,128)(2,1)S(1)} %get-tuple-element.4), channel_id=1, source_target_pairs={{0,1},{1,2},{2,3},{4,5},{5,6},{6,7},{8,9},{9,10},{10,11},{12,13},{... | collective-permute-start | bytes 3538952 | tf_op jit(solution)/shard_map/ppermute | solution.py:10
  42.0 17.9 %collective-permute-start.2 = (bf16[768,768]{1,0:T(8,128)(2,1)S(1)}, bf16[768,768]{1,0:T(8,128)(2,1)}, u32[]{:S(2)}, u32[]{:S(2)}) collective-permute-start(bf16[768,768]{1,0:T(8,128)(2,1)S(1)} %get-tuple-element.4), channel_id=1, source_target_pairs={{1,0},{2,1},{3,2},{5,4},{6,5},{7,6},{9,8},{10,9},{11,10},{13,12},{... | collective-permute-start | bytes 3538952 | tf_op jit(solution)/shard_map/ppermute | solution.py:10
  55.2 1.0 copy-start.3
Sparse Core Ops, SparseCore 0:
  40.1 68.1 reduce-scatter.1
where the time goes:
time: 117 us; the launch traced here: 115 us
  waiting for transfers between devices  71.8 us (61%)
  between operations  14.8 us (13%)
  matrix products  11.7 us (10%)
  starting transfers between devices  11 us (9%)
  other arithmetic  4.9 us (4%)
    reduce_scatter x1, waiting for transfers between devices, shards(): lax.psum_scatter(jnp.dot(left_masked, mixed_block, preferred_element_type...  42.3 us
    ppermute x4, waiting for transfers between devices, passed_along(): return lax.ppermute(block, axis, route)  29.5 us
    ppermute x4, starting transfers between devices, passed_along(): return lax.ppermute(block, axis, route)  11 us
    dot_general x1, matrix products, shards(): lax.dot_general(site_own, carried, (((0,), (0,)), ((), ())), preferred_el...  6.01 us
    dot_general x1, matrix products, shards(): jnp.dot(left_masked, mixed_block, preferred_element_type=jnp.float32)  5.67 us
  transfers between devices with their start and end apart: 5, of which 5 were waited for; matrix products, arithmetic and copies ran while one was open for 6% of the time, Pallas kernels for 0%

commit v1 on v0

v1 whole, which is shorter than its diff:
```python
import functools

import jax
import jax.numpy as jnp
from jax import lax
from jax.experimental import pallas as pl
from jax.experimental.pallas import tpu as pltpu
from jax.sharding import PartitionSpec as P

MESH = pl.DeviceIdType.MESH
BF16 = jnp.bfloat16
F32 = jnp.float32


def flip_bits(number, bits, count):
    out, bit = 0, 1
    while bit < count:
        here = (number // bit) % 2
        out = out + bit * (((here + 1) % 2) if bits & bit else here)
        bit *= 2
    return out


def kernel(
    terms, sectors,
    state, left, right, site, sizes, shift,
    applied, new_left,
    own_s, own_b, lm, rm, mate_s, far_s, mate_b, far_b, bt, mixed, carried,
    kept, y_send, y_recv, z_send, z_recv,
    local_sem, mate_send, mate_recv, x_send_sem, x_recv_sem, relay_send, relay_recv,
    y_send_sem, y_recv_sem, z_send_sem, z_recv_sem,
):
    width = own_s.shape[0]
    depth = terms // 2
    rows = width // terms
    quarter = width // 4
    chunk = quarter // 2
    t, p = lax.axis_index("term"), lax.axis_index("sec")
    z, y = t // 2, t % 2
    odd = p % 2
    mate = p + 1 - 2 * odd
    far = p - 1 + 2 * odd
    has_far = jnp.logical_and(far >= 0, far < sectors)
    far_there = lax.rem(far + sectors, sectors)
    zlow = z % 2
    y_peer = 2 * z + 1 - y
    z_near = 2 * (z + 1 - 2 * zlow) + y
    z_other = [flip_bits(z, depth - 1 - k, depth) for k in range(depth)]

    loads = [
        pltpu.make_async_copy(state.at[0], own_s, local_sem.at[0]),
        pltpu.make_async_copy(left.at[0, 0], lm, local_sem.at[1]),
        pltpu.make_async_copy(right.at[0, 0], rm, local_sem.at[2]),
        pltpu.make_async_copy(site.at[0], own_b, local_sem.at[3]),
    ]
    for load in loads:
        load.start()

    barrier = pltpu.get_barrier_semaphore()
    pl.semaphore_signal(barrier, inc=1, device_id=(t, mate), device_id_type=MESH)

    @pl.when(has_far)
    def _():
        pl.semaphore_signal(barrier, inc=1, device_id=(t, far_there), device_id_type=MESH)

    pl.semaphore_signal(barrier, inc=1, device_id=(y_peer, p), device_id_type=MESH)
    for k in range(depth - 1):
        pl.semaphore_signal(
            barrier, inc=1, device_id=(2 * z_other[k] + y, p), device_id_type=MESH
        )
    pl.semaphore_wait(barrier, depth + 1 + jnp.where(has_far, 1, 0))

    def remote(src, dst, send, recv, device):
        return pltpu.make_async_remote_copy(
            src_ref=src, dst_ref=dst, send_sem=send, recv_sem=recv,
            device_id=device, device_id_type=MESH,
        )

    def part(number, piece=None):
        if piece is None:
            return pl.ds(pl.multiple_of(number * quarter, quarter), quarter)
        return pl.ds(pl.multiple_of(number * quarter + piece * chunk, chunk), chunk)

    q_own = 2 * zlow + y
    q_y = 2 * zlow + 1 - y
    q_z = 2 * (1 - zlow) + y
    q_d = 2 * (1 - zlow) + 1 - y
    there = (t, far_there)
    x_copies = [
        remote(
            state.at[0, part(q_own, i)], far_s.at[part(q_own, i)],
            x_send_sem.at[i], x_recv_sem.at[i], there,
        )
        for i in range(2)
    ]
    x_copies.append(
        remote(
            state.at[0, part(q_d)], far_s.at[part(q_d)],
            x_send_sem.at[2], x_recv_sem.at[2], there,
        )
    )
    x_copies.append(
        remote(site.at[0], far_b, x_send_sem.at[3], x_recv_sem.at[3], there)
    )
    y_relays = [
        remote(
            far_s.at[part(q_own, i)], far_s.at[part(q_own, i)],
            relay_send.at[i], relay_recv.at[i], (y_peer, p),
        )
        for i in range(2)
    ]
    z_relays = [
        remote(
            far_s.at[part(q_own, i)], far_s.at[part(q_own, i)],
            relay_send.at[2 + i], relay_recv.at[2 + i], (z_near, p),
        )
        for i in range(2)
    ]
    y_arrivals = [
        remote(
            far_s.at[part(q_y, i)], far_s.at[part(q_y, i)],
            relay_send.at[i], relay_recv.at[i], (y_peer, p),
        )
        for i in range(2)
    ]
    z_arrivals = [
        remote(
            far_s.at[part(q_z, i)], far_s.at[part(q_z, i)],
            relay_send.at[2 + i], relay_recv.at[2 + i], (z_near, p),
        )
        for i in range(2)
    ]
    mate_copies = [
        remote(state.at[0], mate_s, mate_send.at[0], mate_recv.at[0], (t, mate)),
        remote(site.at[0], mate_b, mate_send.at[1], mate_recv.at[1], (t, mate)),
    ]

    @pl.when(has_far)
    def _():
        for copy in x_copies:
            copy.start()

    for copy in mate_copies:
        copy.start()

    @pl.when(jnp.logical_not(has_far))
    def _():
        far_s[...] = jnp.zeros_like(far_s)
        far_b[...] = jnp.zeros_like(far_b)

    charge_shift = shift[0]
    own_size = jnp.int32(0)
    source_size = jnp.int32(0)
    for i in range(sectors):
        own_size = own_size + jnp.where(p == i, sizes[i], 0)
        source_size = source_size + jnp.where(p + charge_shift == i, sizes[i], 0)
    towards = charge_shift * (1 - 2 * odd)

    def choose(own, near, away):
        return jnp.where(towards == 0, own, jnp.where(towards == 1, near, away))

    loads[2].wait()
    row_ids = lax.broadcasted_iota(jnp.int32, (width, 1), 0)
    rm[...] = rm[...] * jnp.where(row_ids < source_size, 1.0, 0.0).astype(BF16)
    loads[1].wait()
    col_ids = lax.broadcasted_iota(jnp.int32, (1, width), 1)
    lm[...] = lm[...] * jnp.where(col_ids < source_size, 1.0, 0.0).astype(BF16)

    @pl.when(has_far)
    def _():
        for i in range(2):
            x_copies[i].wait_recv()
            y_relays[i].start()
            z_relays[i].start()

    loads[3].wait()
    bt[...] = own_b[...].T
    loads[0].wait()
    mate_copies[0].wait_recv()

    def mix(number):
        where = part(number)
        source = choose(own_s[where, :], mate_s[where, :], far_s[where, :])
        mixed[where, :] = jnp.dot(source, rm[...], preferred_element_type=F32).astype(BF16)

    mix(q_own)

    @pl.when(has_far)
    def _():
        x_copies[2].wait_recv()

    mix(q_d)

    @pl.when(has_far)
    def _():
        for copy in y_arrivals:
            copy.wait_recv()

    mix(q_y)

    @pl.when(has_far)
    def _():
        for copy in z_arrivals:
            copy.wait_recv()

    mix(q_z)

    y_copies, z_copies = [], []
    for k in range(depth):
        start = pl.multiple_of(z_other[k] * 2 * rows, 2 * rows)
        give = pl.ds(pl.multiple_of(start + (1 - y) * rows, rows), rows)
        keep = pl.ds(pl.multiple_of(start + y * rows, rows), rows)
        both = jnp.dot(
            jnp.concatenate([lm[give, :], lm[keep, :]], axis=0), mixed[...],
            preferred_element_type=F32,
        )
        y_send[k] = both[:rows].astype(BF16)
        copy = remote(
            y_send.at[k], y_recv.at[k], y_send_sem.at[k], y_recv_sem.at[k], (y_peer, p)
        )
        copy.start()
        y_copies.append(copy)
        kept[k] = both[rows:]

    for k in range(depth - 1):
        y_copies[k].wait_recv()
        z_send[k] = (kept[k] + y_recv[k].astype(F32)).astype(BF16)
        copy = remote(
            z_send.at[k], z_recv.at[k], z_send_sem.at[k], z_recv_sem.at[k],
            (2 * z_other[k] + y, p),
        )
        copy.start()
        z_copies.append(copy)

    mate_copies[1].wait_recv()

    @pl.when(has_far)
    def _():
        x_copies[3].wait_recv()

    own_b[...] = choose(own_b[...], mate_b[...], far_b[...])
    for i in range(4):
        where = pl.ds(i * quarter, quarter)
        carried[where, :] = jnp.dot(
            lm[where, :], own_b[...], preferred_element_type=F32
        ).astype(BF16)
    row_part = lax.broadcasted_iota(jnp.int32, (width, 1), 0)
    lane_mask = (col_ids < source_size).astype(F32)
    carried[...] = carried[...] * jnp.where(row_part < own_size, 1.0, 0.0).astype(BF16)
    for i in range(4):
        where = pl.ds(i * quarter, quarter)
        renewed = jnp.dot(bt[where, :], carried[...], preferred_element_type=F32)
        ids = lax.broadcasted_iota(jnp.int32, (quarter, 1), 0) + i * quarter
        renewed = renewed * lane_mask * (ids < own_size).astype(F32)
        new_left[0, 0, where, :] = renewed.astype(BF16)

    last = depth - 1
    y_copies[last].wait_recv()
    total = kept[last] + y_recv[last].astype(F32)
    for k in range(depth - 1):
        z_copies[k].wait_recv()
        total = total + z_recv[k].astype(F32)
    ids = lax.broadcasted_iota(jnp.int32, (rows, 1), 0) + t * rows
    keep_rows = (ids < own_size).astype(F32)
    keep_cols = (col_ids < own_size).astype(F32)
    applied[0] = total * keep_rows * keep_cols

    for copy in y_copies + z_copies + mate_copies:
        copy.wait_send()

    @pl.when(has_far)
    def _():
        for copy in x_copies + y_relays + z_relays:
            copy.wait_send()


def shards(terms, sectors, state, left_environment, right_environment, site_blocks,
           sector_sizes, term_shift):
    width = state.shape[1]
    rows = width // terms
    depth = terms // 2
    square = pltpu.VMEM((width, width), BF16)
    any_space = pl.BlockSpec(memory_space=pl.ANY)
    smem = pl.BlockSpec(memory_space=pltpu.SMEM)
    vmem = pl.BlockSpec(memory_space=pltpu.VMEM)
    dma = pltpu.SemaphoreType.DMA
    return pl.pallas_call(
        functools.partial(kernel, terms, sectors),
        out_shape=(
            jax.ShapeDtypeStruct((1, rows, width), F32),
            jax.ShapeDtypeStruct((1, 1, width, width), BF16),
        ),
        in_specs=[any_space] * 4 + [smem] * 2,
        out_specs=(vmem, vmem),
        scratch_shapes=[square] * 11 + [
            pltpu.VMEM((depth, rows, width), F32),
            pltpu.VMEM((depth, rows, width), BF16),
            pltpu.VMEM((depth, rows, width), BF16),
            pltpu.VMEM((depth, rows, width), BF16),
            pltpu.VMEM((depth, rows, width), BF16),
            dma((4,)), dma((2,)), dma((2,)), dma((4,)), dma((4,)), dma((4,)), dma((4,)),
            dma((depth,)), dma((depth,)), dma((depth,)), dma((depth,)),
        ],
        compiler_params=pltpu.CompilerParams(
            collective_id=0, has_side_effects=True, vmem_limit_bytes=48 * 1024 * 1024
        ),
    )(state, left_environment, right_environment, site_blocks, sector_sizes, term_shift)


def solution(mesh):
    placed = (
        P("sec", None, None),
        P("term", "sec", None, None),
        P("term", "sec", None, None),
        P("sec", None, None),
        P(),
        P("term"),
    )
    return jax.shard_map(
        functools.partial(shards, mesh.shape["term"], mesh.shape["sec"]),
        mesh=mesh,
        in_specs=placed,
        out_specs=(P("sec", "term", None), P("term", "sec", None, None)),
        check_vma=False,
    )
```

time: 117 us -> 41.2 us (0.35); the launches traced: 115 us -> 40.9 us
  waiting for transfers between devices: 71.8 us -> 0 us
  Pallas kernels: 0 us -> 32.2 us
  between operations: 14.8 us -> 1.3 us
  matrix products: 11.7 us -> 0 us
  starting transfers between devices: 11 us -> 0 us
  local copies, waits for them, and re-layouts: 1.03 us -> 7.46 us
  other arithmetic: 4.9 us -> 0 us
    reduce_scatter x1 -> x0, waiting for transfers between devices: 42.3 us -> none  [shards(): lax.psum_scatter(jnp.dot(left_masked, mixed_block, preferred_element_type...]
    pallas_call x0 -> x1, Pallas kernels: none -> 32.2 us  [shards(): pl.pallas_call(functools.partial(kernel, terms, sectors), out_shape=(jax....]
    ppermute x4 -> x0, waiting for transfers between devices: 29.5 us -> none  [passed_along(): return lax.ppermute(block, axis, route)]
    dot_general x2 -> x0, matrix products: 11.7 us -> none  [the longest x1 6.01 us: shards(): lax.dot_general(site_own, carried, (((0,), (0,)), ((), ())), preferred_el...]
    ppermute x4 -> x0, starting transfers between devices: 11 us -> none  [passed_along(): return lax.ppermute(block, axis, route)]
    unnamed x8 -> x12, local copies, waits for them, and re-layouts: 1.03 us -> 7.46 us
    select_n x1 -> x0, other arithmetic: 2.32 us -> none  [shards(): site_own = jnp.where(own_square, site_blocks[0], zero_block)]
    reduce_sum x1 -> x0, other arithmetic: 1.31 us -> none  [shards(): jnp.sum(jnp.where(sector_ids == sector + charge_shift, sector_sizes, 0))]
  transfers between devices with their start and end apart: 5 -> 0, of which waited for: 5 -> 0; matrix products, arithmetic and copies ran while one was open for 6% -> 0% of each run, Pallas kernels for 0% -> 0%
where the time goes in v1:
time: 41.2 us; the launch traced here: 40.9 us
  Pallas kernels  32.2 us (78%)
  local copies, waits for them, and re-layouts  7.46 us (18%)
  between operations  1.3 us (3%)
    pallas_call x1, Pallas kernels, shards(): pl.pallas_call(functools.partial(kernel, terms, sectors), out_shape=(jax....  32.2 us
    unnamed x12, local copies, waits for them, and re-layouts  7.46 us

profile of v1, /device:TPU:1, one launch (start us, length us, event | category | flops | bytes accessed | tf_op | source)
XLA Modules:
  0.0 40.9 jit_solution(13129099058156547482)
XLA Ops:
  1.3 0.0 copy-start
  1.3 1.3 %copy-done = bf16[1,768,768]{2,1,0:T(8,128)(2,1)S(1)} copy-done((bf16[1,768,768]{2,1,0:T(8,128)(2,1)S(1)}, bf16[1,768,768]{2,1,0:T(8,128)(2,1)}, u32[]{:S(2)}) %copy-start) | copy-done | bytes 1179672
  2.5 0.0 copy-start.1
  2.6 1.3 %copy-done.1 = bf16[1,1,768,768]{3,2,1,0:T(8,128)(2,1)S(1)} copy-done((bf16[1,1,768,768]{3,2,1,0:T(8,128)(2,1)S(1)}, bf16[1,1,768,768]{3,2,1,0:T(8,128)(2,1)}, u32[]{:S(2)}) %copy-start.1) | copy-done | bytes 1179672
  3.8 0.0 copy-start.2
  3.8 1.3 %copy-done.2 = bf16[1,1,768,768]{3,2,1,0:T(8,128)(2,1)S(1)} copy-done((bf16[1,1,768,768]{3,2,1,0:T(8,128)(2,1)S(1)}, bf16[1,1,768,768]{3,2,1,0:T(8,128)(2,1)}, u32[]{:S(2)}) %copy-start.2) | copy-done | bytes 1179672
  5.1 0.0 copy-start.3
  5.1 1.3 %copy-done.3 = bf16[1,768,768]{2,1,0:T(8,128)(2,1)S(1)} copy-done((bf16[1,768,768]{2,1,0:T(8,128)(2,1)S(1)}, bf16[1,768,768]{2,1,0:T(8,128)(2,1)}, u32[]{:S(2)}) %copy-start.3) | copy-done | bytes 1179672
  6.4 0.0 copy-start.4
  6.4 0.7 %copy-done.4 = s32[4]{0:T(128)S(1)} copy-done((s32[4]{0:T(128)S(1)}, s32[4]{0:T(128)}, u32[]{:S(2)}) %copy-start.4) | copy-done | bytes 40
  7.0 32.2 %shard_map.77 = (f32[1,96,768]{2,1,0:T(8,128)S(1)}, bf16[1,1,768,768]{3,2,1,0:T(8,128)(2,1)S(1)}) custom-call(bf16[1,768,768]{2,1,0:T(8,128)(2,1)S(1)} %copy-done, bf16[1,1,768,768]{3,2,1,0:T(8,128)(2,1)S(1)} %copy-done.1, bf16[1,1,768,768]{3,2,1,0:T(8,128)(2,1)S(1)} %copy-done.2, bf16[1,768,768]{2,1,0:T(8,128)(2,1)S(1)} %copy-done.3, s32[4]{0:T(128)S(1)} %copy-done.4, ...), custom_call_target="tpu_custom_call" | custom-call | tf_op jit(solution)/shard_map/pallas_call | solution.py:287
  39.2 0.7 %copy.11 = f32[1,96,768]{2,1,0:T(8,128)} copy(f32[1,96,768]{2,1,0:T(8,128)S(1)} %get-tuple-element.4) | data formatting | bytes 589824
  39.9 1.0 %copy.12 = bf16[1,1,768,768]{3,2,1,0:T(8,128)(2,1)} copy(bf16[1,1,768,768]{3,2,1,0:T(8,128)(2,1)S(1)} %get-tuple-element.5) | data formatting | bytes 2359296
Async XLA Ops:
  1.3 1.3 %copy-start = (bf16[1,768,768]{2,1,0:T(8,128)(2,1)S(1)}, bf16[1,768,768]{2,1,0:T(8,128)(2,1)}, u32[]{:S(2)}) copy-start(bf16[1,768,768]{2,1,0:T(8,128)(2,1)} %state.1) | copy-start | bytes 3538948
  2.5 1.3 %copy-start.1 = (bf16[1,1,768,768]{3,2,1,0:T(8,128)(2,1)S(1)}, bf16[1,1,768,768]{3,2,1,0:T(8,128)(2,1)}, u32[]{:S(2)}) copy-start(bf16[1,1,768,768]{3,2,1,0:T(8,128)(2,1)} %left.1) | copy-start | bytes 3538948
  3.8 1.3 %copy-start.2 = (bf16[1,1,768,768]{3,2,1,0:T(8,128)(2,1)S(1)}, bf16[1,1,768,768]{3,2,1,0:T(8,128)(2,1)}, u32[]{:S(2)}) copy-start(bf16[1,1,768,768]{3,2,1,0:T(8,128)(2,1)} %right.1) | copy-start | bytes 3538948
  5.1 1.3 %copy-start.3 = (bf16[1,768,768]{2,1,0:T(8,128)(2,1)S(1)}, bf16[1,768,768]{2,1,0:T(8,128)(2,1)}, u32[]{:S(2)}) copy-start(bf16[1,768,768]{2,1,0:T(8,128)(2,1)} %site.1) | copy-start | bytes 3538948
  6.4 0.7 %copy-start.4 = (s32[4]{0:T(128)S(1)}, s32[4]{0:T(128)}, u32[]{:S(2)}) copy-start(s32[4]{0:T(128)} %sizes.1) | copy-start | bytes 52

commit v2 on v1

--- a/solution.py
+++ b/solution.py
@@ -23,11 +23,11 @@
 
 def kernel(
     terms, sectors,
-    state, left, right, site, sizes, shift,
+    state, left, right, site, sizes_there, shift_there,
     applied, new_left,
     own_s, own_b, lm, rm, mate_s, far_s, mate_b, far_b, bt, mixed, carried,
     kept, y_send, y_recv, z_send, z_recv,
-    local_sem, mate_send, mate_recv, x_send_sem, x_recv_sem, relay_send, relay_recv,
+    sizes, shift, local_sem, mate_send, mate_recv, x_send_sem, x_recv_sem, relay_send, relay_recv,
     y_send_sem, y_recv_sem, z_send_sem, z_recv_sem,
 ):
     width = own_s.shape[0]
@@ -52,6 +52,8 @@
         pltpu.make_async_copy(left.at[0, 0], lm, local_sem.at[1]),
         pltpu.make_async_copy(right.at[0, 0], rm, local_sem.at[2]),
         pltpu.make_async_copy(site.at[0], own_b, local_sem.at[3]),
+        pltpu.make_async_copy(sizes_there, sizes, local_sem.at[4]),
+        pltpu.make_async_copy(shift_there, shift, local_sem.at[5]),
     ]
     for load in loads:
         load.start()
@@ -148,6 +150,8 @@
         far_s[...] = jnp.zeros_like(far_s)
         far_b[...] = jnp.zeros_like(far_b)
 
+    loads[4].wait()
+    loads[5].wait()
     charge_shift = shift[0]
     own_size = jnp.int32(0)
     source_size = jnp.int32(0)
@@ -280,17 +284,16 @@
     rows = width // terms
     depth = terms // 2
     square = pltpu.VMEM((width, width), BF16)
-    any_space = pl.BlockSpec(memory_space=pl.ANY)
-    smem = pl.BlockSpec(memory_space=pltpu.SMEM)
+    hbm = pl.BlockSpec(memory_space=pltpu.HBM)
     vmem = pl.BlockSpec(memory_space=pltpu.VMEM)
     dma = pltpu.SemaphoreType.DMA
     return pl.pallas_call(
         functools.partial(kernel, terms, sectors),
         out_shape=(
-            jax.ShapeDtypeStruct((1, rows, width), F32),
-            jax.ShapeDtypeStruct((1, 1, width, width), BF16),
+            pltpu.VMEM((1, rows, width), F32),
+            pltpu.VMEM((1, 1, width, width), BF16),
         ),
-        in_specs=[any_space] * 4 + [smem] * 2,
+        in_specs=[hbm] * 6,
         out_specs=(vmem, vmem),
         scratch_shapes=[square] * 11 + [
             pltpu.VMEM((depth, rows, width), F32),
@@ -298,11 +301,12 @@
             pltpu.VMEM((depth, rows, width), BF16),
             pltpu.VMEM((depth, rows, width), BF16),
             pltpu.VMEM((depth, rows, width), BF16),
-            dma((4,)), dma((2,)), dma((2,)), dma((4,)), dma((4,)), dma((4,)), dma((4,)),
+            pltpu.SMEM((sectors,), jnp.int32), pltpu.SMEM((1,), jnp.int32),
+            dma((6,)), dma((2,)), dma((2,)), dma((4,)), dma((4,)), dma((4,)), dma((4,)),
             dma((depth,)), dma((depth,)), dma((depth,)), dma((depth,)),
         ],
         compiler_params=pltpu.CompilerParams(
-            collective_id=0, has_side_effects=True, vmem_limit_bytes=48 * 1024 * 1024
+            collective_id=0, has_side_effects=True, vmem_limit_bytes=62500 * 1024
         ),
     )(state, left_environment, right_environment, site_blocks, sector_sizes, term_shift)
 

time: 41.2 us -> 34.1 us (0.83)
  local copies, waits for them, and re-layouts: 7.46 us -> 1.73 us
  Pallas kernels: 32.2 us -> 30.9 us
    unnamed x12 -> x2, local copies, waits for them, and re-layouts: 7.46 us -> 1.73 us
    pallas_call x1, Pallas kernels: 32.2 us -> 30.9 us  [shards(): pl.pallas_call(functools.partial(kernel, terms, sectors), out_shape=(pltp...]
where the time goes in v2:
time: 34.1 us; the launch traced here: 33.9 us
  Pallas kernels  30.9 us (91%)
  local copies, waits for them, and re-layouts  1.73 us (5%)
  between operations  1.29 us (4%)
    pallas_call x1, Pallas kernels, shards(): pl.pallas_call(functools.partial(kernel, terms, sectors), out_shape=(pltp...  30.9 us
    unnamed x2, local copies, waits for them, and re-layouts  1.73 us

profile of v2, /device:TPU:1, one launch (start us, length us, event | category | flops | bytes accessed | tf_op | source)
XLA Modules:
  0.0 33.9 jit_solution(15680435423668938648)
XLA Ops:
  1.3 30.9 %shard_map.77 = (f32[1,96,768]{2,1,0:T(8,128)S(1)}, bf16[1,1,768,768]{3,2,1,0:T(8,128)(2,1)S(1)}) custom-call(bf16[1,768,768]{2,1,0:T(8,128)(2,1)} %state.1, bf16[1,1,768,768]{3,2,1,0:T(8,128)(2,1)} %left.1, bf16[1,1,768,768]{3,2,1,0:T(8,128)(2,1)} %right.1, bf16[1,768,768]{2,1,0:T(8,128)(2,1)} %site.1, s32[4]{0:T(128)} %sizes_there.1, s32[1]{0:T(128)S(6)} %copy.12.shift_there), custom_call_target="tpu_custom_call" | custom-call | tf_op jit(solution)/shard_map/pallas_call | solution.py:290
  32.2 0.7 %copy.10 = f32[1,96,768]{2,1,0:T(8,128)} copy(f32[1,96,768]{2,1,0:T(8,128)S(1)} %get-tuple-element.2) | data formatting | bytes 589824
  32.9 1.0 %copy.11 = bf16[1,1,768,768]{3,2,1,0:T(8,128)(2,1)} copy(bf16[1,1,768,768]{3,2,1,0:T(8,128)(2,1)S(1)} %get-tuple-element.3) | data formatting | bytes 2359296

commit v3 on v2

--- a/solution.py
+++ b/solution.py
@@ -25,8 +25,8 @@
     terms, sectors,
     state, left, right, site, sizes_there, shift_there,
     applied, new_left,
-    own_s, own_b, lm, rm, mate_s, far_s, mate_b, far_b, bt, mixed, carried,
-    kept, y_send, y_recv, z_send, z_recv,
+    own_s, own_b, lm, rm, mate_s, far_s, mate_b, far_b, bt, mixed, weight,
+    acc, kept, y_send, y_recv, z_send, z_recv,
     sizes, shift, local_sem, mate_send, mate_recv, x_send_sem, x_recv_sem, relay_send, relay_recv,
     y_send_sem, y_recv_sem, z_send_sem, z_recv_sem,
 ):
@@ -45,7 +45,10 @@
     zlow = z % 2
     y_peer = 2 * z + 1 - y
     z_near = 2 * (z + 1 - 2 * zlow) + y
-    z_other = [flip_bits(z, depth - 1 - k, depth) for k in range(depth)]
+    even = [h for h in range(1, depth) if bin(h).count("1") % 2 == 0]
+    order = [1 ^ h for h in even] + [1] + even + [0]
+    z_other = [flip_bits(z, mask, depth) for mask in order]
+    neighbours = len(even) + 1
 
     loads = [
         pltpu.make_async_copy(state.at[0], own_s, local_sem.at[0]),
@@ -66,11 +69,17 @@
         pl.semaphore_signal(barrier, inc=1, device_id=(t, far_there), device_id_type=MESH)
 
     pl.semaphore_signal(barrier, inc=1, device_id=(y_peer, p), device_id_type=MESH)
-    for k in range(depth - 1):
+    for k in range(neighbours - 1, depth - 1):
         pl.semaphore_signal(
             barrier, inc=1, device_id=(2 * z_other[k] + y, p), device_id_type=MESH
         )
-    pl.semaphore_wait(barrier, depth + 1 + jnp.where(has_far, 1, 0))
+
+    @pl.when(jnp.logical_not(has_far))
+    def _():
+        far_s[...] = jnp.zeros_like(far_s)
+        far_b[...] = jnp.zeros_like(far_b)
+
+    pl.semaphore_wait(barrier, neighbours + 2 + jnp.where(has_far, 1, 0))
 
     def remote(src, dst, send, recv, device):
         return pltpu.make_async_remote_copy(
@@ -101,15 +110,25 @@
             x_send_sem.at[2], x_recv_sem.at[2], there,
         )
     )
-    x_copies.append(
-        remote(site.at[0], far_b, x_send_sem.at[3], x_recv_sem.at[3], there)
+    x_state = remote(
+        state.at[0, part(q_y, 1)], far_s.at[part(q_y, 1)],
+        x_send_sem.at[5], x_recv_sem.at[5], there,
     )
+    late = 2 * (width // 3)
+    site_parts = [pl.ds(0, late), pl.ds(late, width - late)]
+    for i, rows_of in enumerate(site_parts):
+        x_copies.append(
+            remote(
+                site.at[0, rows_of], far_b.at[rows_of],
+                x_send_sem.at[3 + i], x_recv_sem.at[3 + i], there,
+            )
+        )
     y_relays = [
         remote(
             far_s.at[part(q_own, i)], far_s.at[part(q_own, i)],
             relay_send.at[i], relay_recv.at[i], (y_peer, p),
         )
-        for i in range(2)
+        for i in range(1)
     ]
     z_relays = [
         remote(
@@ -123,7 +142,7 @@
             far_s.at[part(q_y, i)], far_s.at[part(q_y, i)],
             relay_send.at[i], relay_recv.at[i], (y_peer, p),
         )
-        for i in range(2)
+        for i in range(1)
     ]
     z_arrivals = [
         remote(
@@ -133,22 +152,21 @@
         for i in range(2)
     ]
     mate_copies = [
-        remote(state.at[0], mate_s, mate_send.at[0], mate_recv.at[0], (t, mate)),
-        remote(site.at[0], mate_b, mate_send.at[1], mate_recv.at[1], (t, mate)),
-    ]
-
-    @pl.when(has_far)
-    def _():
-        for copy in x_copies:
+        remote(
+            state.at[0, part(q)], mate_s.at[part(q)], mate_send.at[i], mate_recv.at[i],
+            (t, mate),
+        )
+        for i, q in enumerate((q_own, q_d, q_y, q_z))
+    ]
+    mate_site = remote(site.at[0], mate_b, mate_send.at[4], mate_recv.at[4], (t, mate))
+
+    @pl.when(has_far)
+    def _():
+        for copy in x_copies[:3] + [x_state] + x_copies[3:]:
             copy.start()
 
     for copy in mate_copies:
         copy.start()
-
-    @pl.when(jnp.logical_not(has_far))
-    def _():
-        far_s[...] = jnp.zeros_like(far_s)
-        far_b[...] = jnp.zeros_like(far_b)
 
     loads[4].wait()
     loads[5].wait()
@@ -174,40 +192,40 @@
     def _():
         for i in range(2):
             x_copies[i].wait_recv()
-            y_relays[i].start()
+            if i == 0:
+                y_relays[i].start()
             z_relays[i].start()
 
-    loads[3].wait()
-    bt[...] = own_b[...].T
     loads[0].wait()
-    mate_copies[0].wait_recv()
-
-    def mix(number):
+    def mix(i, number):
+        mate_copies[i].wait_recv()
         where = part(number)
         source = choose(own_s[where, :], mate_s[where, :], far_s[where, :])
         mixed[where, :] = jnp.dot(source, rm[...], preferred_element_type=F32).astype(BF16)
 
-    mix(q_own)
+    mix(0, q_own)
 
     @pl.when(has_far)
     def _():
         x_copies[2].wait_recv()
 
-    mix(q_d)
-
-    @pl.when(has_far)
-    def _():
+    mix(1, q_d)
+
+    @pl.when(has_far)
+    def _():
+        x_state.wait_recv()
         for copy in y_arrivals:
             copy.wait_recv()
 
-    mix(q_y)
+    mix(2, q_y)
 
     @pl.when(has_far)
     def _():
         for copy in z_arrivals:
             copy.wait_recv()
 
-    mix(q_z)
+    mix(3, q_z)
+    mate_site.start()
 
     y_copies, z_copies = [], []
     for k in range(depth):
@@ -226,42 +244,65 @@
         y_copies.append(copy)
         kept[k] = both[rows:]
 
+    loads[3].wait()
+    own_rows = (row_ids < own_size).astype(F32)
+    bt[...] = (own_b[...] * own_rows.astype(BF16)).T
+    for i in range(4):
+        where = pl.ds(i * quarter, quarter)
+        weight[where, :] = jnp.dot(
+            bt[where, :], lm[...], preferred_element_type=F32
+        ).astype(BF16)
+
     for k in range(depth - 1):
         y_copies[k].wait_recv()
-        z_send[k] = (kept[k] + y_recv[k].astype(F32)).astype(BF16)
+        value = kept[k] + y_recv[k].astype(F32)
+        if k >= neighbours:
+            z_copies[k - neighbours].wait_recv()
+            value = value + z_recv[k - neighbours].astype(F32)
+        z_send[k] = value.astype(BF16)
+        peer = z_near if k < neighbours else 2 * z_other[k] + y
         copy = remote(
-            z_send.at[k], z_recv.at[k], z_send_sem.at[k], z_recv_sem.at[k],
-            (2 * z_other[k] + y, p),
+            z_send.at[k], z_recv.at[k], z_send_sem.at[k], z_recv_sem.at[k], (peer, p)
         )
         copy.start()
         z_copies.append(copy)
 
-    mate_copies[1].wait_recv()
+    mate_site.wait_recv()
 
     @pl.when(has_far)
     def _():
         x_copies[3].wait_recv()
 
-    own_b[...] = choose(own_b[...], mate_b[...], far_b[...])
+    early = pl.ds(0, late)
+    own_b[early, :] = choose(own_b[early, :], mate_b[early, :], far_b[early, :])
     for i in range(4):
         where = pl.ds(i * quarter, quarter)
-        carried[where, :] = jnp.dot(
-            lm[where, :], own_b[...], preferred_element_type=F32
-        ).astype(BF16)
-    row_part = lax.broadcasted_iota(jnp.int32, (width, 1), 0)
+        acc[where, :] = jnp.dot(
+            weight[where, early], own_b[early, :], preferred_element_type=F32
+        )
+
+    last = depth - 1
+    y_copies[last].wait_recv()
+    kept[last] = kept[last] + y_recv[last].astype(F32)
+
+    @pl.when(has_far)
+    def _():
+        x_copies[4].wait_recv()
+
+    rest = pl.ds(late, width - late)
     lane_mask = (col_ids < source_size).astype(F32)
-    carried[...] = carried[...] * jnp.where(row_part < own_size, 1.0, 0.0).astype(BF16)
+    tail = choose(own_b[rest, :], mate_b[rest, :], far_b[rest, :])
     for i in range(4):
         where = pl.ds(i * quarter, quarter)
-        renewed = jnp.dot(bt[where, :], carried[...], preferred_element_type=F32)
+        renewed = acc[where, :] + jnp.dot(
+            weight[where, rest], tail, preferred_element_type=F32
+        )
         ids = lax.broadcasted_iota(jnp.int32, (quarter, 1), 0) + i * quarter
         renewed = renewed * lane_mask * (ids < own_size).astype(F32)
         new_left[0, 0, where, :] = renewed.astype(BF16)
 
-    last = depth - 1
-    y_copies[last].wait_recv()
-    total = kept[last] + y_recv[last].astype(F32)
-    for k in range(depth - 1):
+    total = kept[last]
+    for k in range(neighbours - 1, depth - 1):
         z_copies[k].wait_recv()
         total = total + z_recv[k].astype(F32)
     ids = lax.broadcasted_iota(jnp.int32, (rows, 1), 0) + t * rows
@@ -269,12 +310,12 @@
     keep_cols = (col_ids < own_size).astype(F32)
     applied[0] = total * keep_rows * keep_cols
 
-    for copy in y_copies + z_copies + mate_copies:
+    for copy in y_copies + z_copies + mate_copies + [mate_site]:
         copy.wait_send()
 
     @pl.when(has_far)
     def _():
-        for copy in x_copies + y_relays + z_relays:
+        for copy in x_copies + [x_state] + y_relays + z_relays:
             copy.wait_send()
 
 
@@ -296,13 +337,14 @@
         in_specs=[hbm] * 6,
         out_specs=(vmem, vmem),
         scratch_shapes=[square] * 11 + [
+            pltpu.VMEM((width, width), F32),
             pltpu.VMEM((depth, rows, width), F32),
             pltpu.VMEM((depth, rows, width), BF16),
             pltpu.VMEM((depth, rows, width), BF16),
             pltpu.VMEM((depth, rows, width), BF16),
             pltpu.VMEM((depth, rows, width), BF16),
             pltpu.SMEM((sectors,), jnp.int32), pltpu.SMEM((1,), jnp.int32),
-            dma((6,)), dma((2,)), dma((2,)), dma((4,)), dma((4,)), dma((4,)), dma((4,)),
+            dma((6,)), dma((5,)), dma((5,)), dma((6,)), dma((6,)), dma((4,)), dma((4,)),
             dma((depth,)), dma((depth,)), dma((depth,)), dma((depth,)),
         ],
         compiler_params=pltpu.CompilerParams(

time: 34.1 us -> 32.5 us (0.953)
  Pallas kernels: 30.9 us -> 29.3 us
    pallas_call x1, Pallas kernels: 30.9 us -> 29.3 us  [shards(): pl.pallas_call(functools.partial(kernel, terms, sectors), out_shape=(pltp...]
where the time goes in v3:
time: 32.5 us; the launch traced here: 32.4 us
  Pallas kernels  29.3 us (90%)
  local copies, waits for them, and re-layouts  1.73 us (5%)
  between operations  1.29 us (4%)
    pallas_call x1, Pallas kernels, shards(): pl.pallas_call(functools.partial(kernel, terms, sectors), out_shape=(pltp...  29.3 us
    unnamed x2, local copies, waits for them, and re-layouts  1.73 us

profile of v3, /device:TPU:1, one launch (start us, length us, event | category | flops | bytes accessed | tf_op | source)
XLA Modules:
  0.0 32.4 jit_solution(3232315511696657743)
XLA Ops:
  1.3 29.3 %shard_map.77 = (f32[1,96,768]{2,1,0:T(8,128)S(1)}, bf16[1,1,768,768]{3,2,1,0:T(8,128)(2,1)S(1)}) custom-call(bf16[1,768,768]{2,1,0:T(8,128)(2,1)} %state.1, bf16[1,1,768,768]{3,2,1,0:T(8,128)(2,1)} %left.1, bf16[1,1,768,768]{3,2,1,0:T(8,128)(2,1)} %right.1, bf16[1,768,768]{2,1,0:T(8,128)(2,1)} %site.1, s32[4]{0:T(128)} %sizes_there.1, s32[1]{0:T(128)S(6)} %copy.12.shift_there), custom_call_target="tpu_custom_call" | custom-call | tf_op jit(solution)/shard_map/pallas_call | solution.py:331
  30.6 0.7 %copy.10 = f32[1,96,768]{2,1,0:T(8,128)} copy(f32[1,96,768]{2,1,0:T(8,128)S(1)} %get-tuple-element.2) | data formatting | bytes 589824
  31.3 1.0 %copy.11 = bf16[1,1,768,768]{3,2,1,0:T(8,128)(2,1)} copy(bf16[1,1,768,768]{3,2,1,0:T(8,128)(2,1)S(1)} %get-tuple-element.3) | data formatting | bytes 2359296
